TPU v7x, 32 devices: a whole 2x2x4 slice. The times are simulated.
32 devices in a mesh: tile: 4 (over y, x), mom: 2 (over core), ewin: 4 (over z).
Axes of the slice: x: 2, y: 2, z: 4, core: 2. Of those that a mesh axis runs over, the one named last changes fastest.
Arguments:
- green_ret: bfloat16 [2, 4, 4, 512, 1024], P('mom', 'ewin', 'tile'), may hold values from -0.25 to 0.25
- injection: float32 [2, 4, 4, 512], P('mom', 'ewin', 'tile'), may hold values from 0.1 to 1
- mom_shift: int32 [4], replicated, may hold values from 0 to 7, as said below
- phon_off: int32 [8], replicated, may hold values from -4 to 4
- coupling: float32 [4, 8], replicated, may hold values from 0.05 to 1
- tile_nbr: int32 [4, 4], replicated, may hold values from 0 to 3
Outputs:
- sigma_less: bfloat16 [2, 4, 4, 512, 1024], P('mom', 'ewin', None, 'tile')
Inputs may be any that keep to these rules, and one draw needn't show every extreme that they name: `mom_shift`: every residue from 0 to 1 appears among the 4 shifts taken modulo 2.
All inputs are finite; a program needn't handle non-finite values.
Results may differ from a plain program's by a relative error of at most 0.0036.
Values may be sent and summed in bfloat16 or wider, within the bound.
A program may use at most 64 MiB of HBM per device.

v0:
```python
import jax
import jax.numpy as jnp
from jax import lax
from jax.sharding import PartitionSpec as P

HW = 4
NW = 8


def with_halo(shard, sides, width):
    for axis, dim in sides:
        peers, length = (lax.axis_size(axis), shard.shape[dim])
        up = [(i, (i + 1) % peers) for i in range(peers - 1)]
        down = [(j, i) for i, j in up]
        last = lax.slice_in_dim(shard, length - width, length, axis=dim)
        initial = lax.slice_in_dim(shard, 0, width, axis=dim)
        before = lax.ppermute(last, axis, up)
        after = lax.ppermute(initial, axis, down)
        shard = jnp.concatenate([before, shard, after], axis=dim)
    return shard


def on_device(green_ret, injection, mom_shift, phon_off, coupling, tile_nbr):
    blocks = green_ret[0, 0]
    gamma = injection[0, 0]
    orbitals = blocks.shape[1]
    ntiles = lax.axis_size("tile")
    per_tile = orbitals // ntiles
    real_part = blocks[:, :, :orbitals].astype(jnp.float32)
    imag_part = blocks[:, :, orbitals:].astype(jnp.float32)
    scale = gamma[:, None, :]
    left_re = jnp.concatenate([real_part * scale, imag_part * scale], axis=2).astype(jnp.bfloat16)
    left_im = jnp.concatenate([imag_part * scale, -real_part * scale], axis=2).astype(jnp.bfloat16)
    real_out = jnp.einsum("prk,pck->prc", left_re, blocks, preferred_element_type=jnp.float32)
    imag_out = jnp.einsum("prk,pck->prc", left_im, blocks, preferred_element_type=jnp.float32)
    payload = jnp.concatenate([real_out, imag_out], axis=2).astype(jnp.bfloat16)
    exchanged = lax.all_to_all(payload, "tile", split_axis=1, concat_axis=0, tiled=True)
    energies = exchanged.shape[0]
    rimmed = with_halo(exchanged, (("ewin", 0),), HW)
    extended = lax.all_gather(rimmed[None], "mom", axis=0, tiled=True)
    nmom = lax.axis_size("mom")
    here = lax.axis_index("mom")
    source = jnp.mod(here - mom_shift, nmom)
    onehot = (source[:, None] == jnp.arange(nmom, dtype=jnp.int32)[None, :]).astype(jnp.float32)
    weights = jnp.dot(onehot.T, coupling, precision=lax.Precision.HIGHEST)
    total = jnp.zeros(exchanged.shape, jnp.float32)
    for offset in range(NW):
        start = HW + phon_off[offset]
        piece = lax.dynamic_slice_in_dim(extended, start, energies, 1)
        for moment in range(nmom):
            total = total + weights[moment, offset] * piece[moment].astype(jnp.float32)
    tile_here = lax.axis_index("tile")
    neighbours = lax.dynamic_index_in_dim(tile_nbr, tile_here, 0, keepdims=False)
    coltile = jnp.arange(orbitals, dtype=jnp.int32) // per_tile
    colmask = jnp.any(coltile[:, None] == neighbours[None, :], axis=1).astype(jnp.float32)
    colmask = jnp.concatenate([colmask, colmask])
    result = (total * colmask[None, None, :]).astype(jnp.bfloat16)
    return result[None, None]


def solution(mesh):
    placed = (
        P("mom", "ewin", "tile", None, None),
        P("mom", "ewin", "tile", None),
        P(),
        P(),
        P(),
        P(),
    )
    return jax.shard_map(
        on_device,
        mesh=mesh,
        in_specs=placed,
        out_specs=P("mom", "ewin", None, "tile", None),
        check_vma=False,
    )
```

profile of v0, /device:TPU:0, one launch (start us, length us, event | category | flops | bytes accessed | tf_op | source)
XLA Modules:
  0.0 113.0 jit_solution(7186449994337882947)
XLA Ops:
  6.5 0.0 copy-start
  6.5 0.0 copy-start.1
  6.5 0.0 all-gather.3.cloned.1.call-start
  6.5 1.6 %fusion.17 = (bf16[512,512]{1,0:T(8,128)(2,1)S(1)}, bf16[512,512]{1,0:T(8,128)(2,1)S(1)}, bf16[512,512]{1,0:T(8,128)(2,1)S(1)}) fusion(f32[512]{0:T(512)} %bitcast.71, bf16[1,512,1024]{2,1,0:T(8,128)(2,1)} %bitcast.70), kind=kLoop, calls=%fused_computation.25 | loop fusion | flops 2359296 | bytes 2623488 | tf_op jit(solution)/shard_map/concatenate | solution.py:32
  8.2 0.0 copy-done.1
  8.2 0.7 fusion.2
  8.9 0.7 fusion.3
  9.7 0.1 pad_maximum_fusion.1
  9.8 2.0 %copy.10 = bf16[1,512,1024]{2,0,1:T(2,128)(2,1)S(1)} copy(bf16[1,512,1024]{1,2,0:T(8,128)(2,1)S(1)} %pad_maximum_fusion.1) | data formatting | bytes 2097152 | tf_op jit(solution)/shard_map/concatenate | solution.py:36
  11.7 0.5 broadcast.191
  12.3 7.3 %reduce = bf16[512,1024]{1,0:T(8,128)(2,1)S(1)} reduce(bf16[512,1,1024]{2,1,0:T(2,128)(2,1)S(1)} %bitcast.66, bf16[]{:T(256)} %broadcast.191), dimensions={1}, to_apply=%bitcast.61.reduce_sub_computation | reduce | bytes 2097154
  19.6 0.8 reshape.449
  20.4 19.1 %all_to_all.12 = bf16[4,2,65536]{2,1,0:T(2,128)(2,1)S(1)} all-to-all(bf16[4,2,65536]{2,1,0:T(2,128)(2,1)S(1)} %reshape.449), channel_id=1, replica_groups=mesh['tile'=4,'mom'=2,'ewin'=4] {'tile'}, dimensions={0} | all-to-all | bytes 2097152 | tf_op jit(solution)/shard_map/all_to_all | solution.py:37
  39.5 0.9 reshape.450
  40.5 0.4 copy.11
  40.9 3.5 %collective-permute-start = (bf16[4,128,1024]{2,1,0:T(8,128)(2,1)S(1)}, bf16[4,128,1024]{2,1,0:T(8,128)(2,1)S(1)}, u32[]{:S(2)}, u32[]{:S(2)}) collective-permute-start(bf16[4,128,1024]{2,1,0:T(8,128)(2,1)S(1)} %bitcast.67), channel_id=1, source_target_pairs={{0,1},{1,2},{2,3},{4,5},{5,6},{6,7},{8,9},{9,10},{10,11},{12,13},{... | collective-permute-start | bytes 3145736 | tf_op jit(solution)/shard_map/ppermute | solution.py:17
  44.4 1.5 %collective-permute-start.1 = (bf16[4,128,1024]{2,1,0:T(8,128)(2,1)S(1)}, bf16[4,128,1024]{2,1,0:T(8,128)(2,1)S(1)}, u32[]{:S(2)}, u32[]{:S(2)}) collective-permute-start(bf16[4,128,1024]{2,1,0:T(8,128)(2,1)S(1)} %bitcast.68), channel_id=1, source_target_pairs={{1,0},{2,1},{3,2},{5,4},{6,5},{7,6},{9,8},{10,9},{11,10},{13,12},{... | collective-permute-start | bytes 3145736 | tf_op jit(solution)/shard_map/ppermute | solution.py:18
  45.9 19.4 %collective-permute-done = bf16[4,128,1024]{2,1,0:T(8,128)(2,1)S(1)} collective-permute-done((bf16[4,128,1024]{2,1,0:T(8,128)(2,1)S(1)}, bf16[4,128,1024]{2,1,0:T(8,128)(2,1)S(1)}, u32[]{:S(2)}, u32[]{:S(2)}) %collective-permute-start) | collective-permute-done | bytes 1048608 | tf_op jit(solution)/shard_map/ppermute | solution.py:17
  65.2 4.2 %collective-permute-done.1 = bf16[4,128,1024]{2,1,0:T(8,128)(2,1)S(1)} collective-permute-done((bf16[4,128,1024]{2,1,0:T(8,128)(2,1)S(1)}, bf16[4,128,1024]{2,1,0:T(8,128)(2,1)S(1)}, u32[]{:S(2)}, u32[]{:S(2)}) %collective-permute-start.1) | collective-permute-done | bytes 1048608 | tf_op jit(solution)/shard_map/ppermute | solution.py:18
  69.4 1.8 %pad_maximum_fusion = bf16[12,128,1024]{2,1,0:T(8,128)(2,1)} fusion(bf16[4,128,1024]{2,1,0:T(8,128)(2,1)S(1)} %collective-permute-done.1, bf16[4,128,1024]{2,1,0:T(8,128)(2,1)S(1)} %bitcast.69, bf16[4,128,1024]{2,1,0:T(8,128)(2,1)S(1)} %collective-permute-done), kind=kLoop, calls=%fused_computation | loop fusion | flops 3145728 | bytes 6291456 | tf_op jit(solution)/shard_map/concatenate | solution.py:19
  71.3 0.0 copy-start.2
  71.3 0.0 copy-start.3
  71.3 0.0 all-gather.3.cloned.1.call-update
  71.3 0.6 copy-done.2
  71.9 0.7 fusion.28
  82.8 0.7 fusion.24
  83.6 0.1 compare_reduce_fusion
  83.7 0.0 copy-done.3
  83.7 0.0 copy-done
  83.7 0.3 fusion.21
  83.9 0.7 fusion.27
  84.6 2.6 %all-gather.3.cloned.1.call-done = bf16[24,128,1024]{2,1,0:T(8,128)(2,1)} async-done(((bf16[12,128,1024]{2,1,0:T(8,128)(2,1)}), bf16[24,128,1024]{2,1,0:T(8,128)(2,1)}) %all-gather.3.cloned.1.call-update) | async-done | bytes 6291472 | tf_op jit(solution)/shard_map/all_gather | solution.py:40
  87.2 19.0 %fusion.1 = bf16[1,1,4,128,1024]{4,3,2,1,0:T(8,128)(2,1)} fusion(bf16[2,12,128,1024]{3,2,1,0:T(8,128)(2,1)} %bitcast.64, s32[]{:T(128)S(6)} %add.344, s32[]{:T(128)S(6)} %select_n.52, s32[]{:T(128)S(6)} %select_n.51, s32[]{:T(128)S(6)} %select_n.50, s32[]{:T(128)S(6)} %select_n.49, s32[]{:T(128)S(6)} %select_n.48, s32[]{:T(128)S(6)} %select_n.47, ...), kind=kLoop, calls=%fused_computation.3 | loop fusion | flops 25690112 | bytes 17829988 | tf_op jit(solution)/shard_map/convert_element_type | solution.py:57
  (3 shorter events, 0.0 us)
Async XLA Ops:
  6.5 77.2 %copy-start = (f32[4,8]{1,0:T(4,128)S(1)}, f32[4,8]{1,0:T(4,128)}, u32[]{:S(2)}) copy-start(f32[4,8]{1,0:T(4,128)} %param.10) | copy-start | bytes 388
  6.5 1.6 %copy-start.1 = (bf16[1,1,1,512,1024]{4,3,2,1,0:T(8,128)(2,1)S(1)}, bf16[1,1,1,512,1024]{4,3,2,1,0:T(8,128)(2,1)}, u32[]{:S(2)}) copy-start(bf16[1,1,1,512,1024]{4,3,2,1,0:T(8,128)(2,1)} %param.6) | copy-start | bytes 3145732
  6.5 80.7 %all-gather.3.cloned.1.call-start = ((), (), s32[]{:S(2)}) async-start(), calls=%async_computation.1 | async-start | bytes 9437184 | tf_op jit(solution)/shard_map/all_gather | solution.py:40
  40.9 24.4 %collective-permute-start = (bf16[4,128,1024]{2,1,0:T(8,128)(2,1)S(1)}, bf16[4,128,1024]{2,1,0:T(8,128)(2,1)S(1)}, u32[]{:S(2)}, u32[]{:S(2)}) collective-permute-start(bf16[4,128,1024]{2,1,0:T(8,128)(2,1)S(1)} %bitcast.67), channel_id=1, source_target_pairs={{0,1},{1,2},{2,3},{4,5},{5,6},{6,7},{8,9},{9,10},{10,11},{12,13},{... | collective-permute-start | bytes 3145736 | tf_op jit(solution)/shard_map/ppermute | solution.py:17
  44.4 25.0 %collective-permute-start.1 = (bf16[4,128,1024]{2,1,0:T(8,128)(2,1)S(1)}, bf16[4,128,1024]{2,1,0:T(8,128)(2,1)S(1)}, u32[]{:S(2)}, u32[]{:S(2)}) collective-permute-start(bf16[4,128,1024]{2,1,0:T(8,128)(2,1)S(1)} %bitcast.68), channel_id=1, source_target_pairs={{1,0},{2,1},{3,2},{5,4},{6,5},{7,6},{9,8},{10,9},{11,10},{13,12},{... | collective-permute-start | bytes 3145736 | tf_op jit(solution)/shard_map/ppermute | solution.py:18
  71.3 0.7 copy-start.2
  71.3 12.4 %copy-start.3 = (s32[4]{0:T(128)S(1)}, s32[4]{0:T(128)}, u32[]{:S(2)}) copy-start(s32[4]{0:T(128)} %param.8) | copy-start | bytes 52
Sparse Core Ops, SparseCore 0:
  71.4 15.7 all-gather.2
where the time goes:
time: 114 us; the launch traced here: 113 us
  other arithmetic  29.9 us (26%)
  waiting for transfers between devices  26.1 us (23%)
  between operations  23.8 us (21%)
  blocking collectives  19.1 us (17%)
  local copies, waits for them, and re-layouts  7.35 us (6%)
  starting transfers between devices  5.01 us (4%)
  matrix products  1.74 us (2%)
    ppermute x1, waiting for transfers between devices, with_halo(): before = lax.ppermute(last, axis, up)  19.4 us
    all_to_all x1, blocking collectives, on_device(): lax.all_to_all(payload, 'tile', split_axis=1, concat_axis=0, tiled=True)  19.1 us
    convert_element_type x1, other arithmetic, on_device(): result = (total * colmask[None, None, :]).astype(jnp.bfloat16)  19 us
    unnamed x1, other arithmetic  7.31 us
    ppermute x1, waiting for transfers between devices, with_halo(): after = lax.ppermute(initial, axis, down)  4.18 us
    ppermute x1, starting transfers between devices, with_halo(): before = lax.ppermute(last, axis, up)  3.54 us
    unnamed x12, local copies, waits for them, and re-layouts  3.28 us
    all_gather x1, waiting for transfers between devices, on_device(): extended = lax.all_gather(rimmed[None], 'mom', axis=0, tiled=True)  2.56 us
  transfers between devices with their start and end apart: 3, of which 3 were waited for; matrix products, arithmetic and copies ran while one was open for 2% of the time, Pallas kernels for 0%

commit v1 on v0

--- a/solution.py
+++ b/solution.py
@@ -1,3 +1,4 @@
+import functools
 import jax
 import jax.numpy as jnp
 from jax import lax
@@ -5,6 +6,18 @@
 
 HW = 4
 NW = 8
+
+
+def _prepare_files(my_data, which_axis):
+    return jnp.concatenate(
+        lax.all_to_all(
+            jnp.stack(jnp.split(my_data, lax.psum(1, which_axis), axis=1), axis=0), which_axis, 0, 0
+        ),
+        axis=0,
+    )
+
+
+define_views = functools.partial(_prepare_files, which_axis="tile")
 
 
 def with_halo(shard, sides, width):
@@ -34,7 +47,7 @@
     real_out = jnp.einsum("prk,pck->prc", left_re, blocks, preferred_element_type=jnp.float32)
     imag_out = jnp.einsum("prk,pck->prc", left_im, blocks, preferred_element_type=jnp.float32)
     payload = jnp.concatenate([real_out, imag_out], axis=2).astype(jnp.bfloat16)
-    exchanged = lax.all_to_all(payload, "tile", split_axis=1, concat_axis=0, tiled=True)
+    exchanged = define_views(payload)
     energies = exchanged.shape[0]
     rimmed = with_halo(exchanged, (("ewin", 0),), HW)
     extended = lax.all_gather(rimmed[None], "mom", axis=0, tiled=True)

time: 114 us -> 103 us (0.904)
  other arithmetic: 29.9 us -> 21.4 us
  local copies, waits for them, and re-layouts: 7.35 us -> 5.64 us
    unnamed x1 -> x0, other arithmetic: 7.31 us -> none
    unnamed x12 -> x8, local copies, waits for them, and re-layouts: 3.28 us -> 0.64 us
    concatenate x1, other arithmetic: 1.83 us -> 0.37 us  [with_halo(): shard = jnp.concatenate([before, shard, after], axis=dim)]
where the time goes in v1:
time: 103 us
  waiting for transfers between devices  26.7 us (26%)
  between operations  23.3 us (23%)
  other arithmetic  21.4 us (21%)
  blocking collectives  19.1 us (19%)
  local copies, waits for them, and re-layouts  5.64 us (5%)
  starting transfers between devices  4.83 us (5%)
  matrix products  1.74 us (2%)
    ppermute x1, waiting for transfers between devices, with_halo(): before = lax.ppermute(last, axis, up)  19.5 us
    all_to_all x1, blocking collectives, _prepare_files(): lax.all_to_all(jnp.stack(jnp.split(my_data, lax.psum(1, which_axis), axis...  19.1 us
    convert_element_type x1, other arithmetic, on_device(): result = (total * colmask[None, None, :]).astype(jnp.bfloat16)  19 us
    ppermute x1, waiting for transfers between devices, with_halo(): after = lax.ppermute(initial, axis, down)  4.18 us
    ppermute x1, starting transfers between devices, with_halo(): before = lax.ppermute(last, axis, up)  3.54 us
    all_gather x1, waiting for transfers between devices, on_device(): extended = lax.all_gather(rimmed[None], 'mom', axis=0, tiled=True)  3 us
    concatenate x1, local copies, waits for them, and re-layouts, with_halo(): shard = jnp.concatenate([before, shard, after], axis=dim)  2.91 us
  transfers between devices with their start and end apart: 3, of which 3 were waited for; matrix products, arithmetic and copies ran while one was open for 2% of the time, Pallas kernels for 0%

profile of v1, /device:TPU:0, one launch (start us, length us, event | category | flops | bytes accessed | tf_op | source)
XLA Modules:
  0.0 102.8 jit_solution(127673633655513251)
XLA Ops:
  6.5 0.0 copy-start
  6.5 0.0 copy-start.1
  6.5 0.0 all-gather.3.cloned.1.call-start
  6.5 1.6 %fusion.17 = (bf16[512,512]{1,0:T(8,128)(2,1)S(1)}, bf16[512,512]{1,0:T(8,128)(2,1)S(1)}, bf16[512,512]{1,0:T(8,128)(2,1)S(1)}) fusion(f32[512]{0:T(512)} %bitcast.75, bf16[1,512,1024]{2,1,0:T(8,128)(2,1)} %bitcast.74), kind=kLoop, calls=%fused_computation.31 | loop fusion | flops 2359296 | bytes 2623488 | tf_op jit(solution)/shard_map/concatenate | solution.py:45
  8.2 0.0 copy-done.1
  8.2 0.7 fusion.3
  8.9 0.7 fusion.2
  9.7 0.2 fusion.21
  9.9 0.1 pad_maximum_fusion.1
  10.0 19.1 %all_to_all.5 = bf16[4,1,128,1024]{2,3,1,0:T(8,128)(2,1)S(1)} all-to-all(bf16[4,1,128,1024]{2,3,1,0:T(8,128)(2,1)S(1)} %pad_maximum_fusion.1), channel_id=1, replica_groups=mesh['tile'=4,'mom'=2,'ewin'=4] {'tile'}, dimensions={0} | all-to-all | bytes 2097152 | tf_op jit(solution)/shard_map/all_to_all | solution.py:13
  29.1 3.5 %collective-permute-start = (bf16[4,128,1024]{1,2,0:T(8,128)(2,1)S(1)}, bf16[4,128,1024]{1,2,0:T(8,128)(2,1)S(1)}, u32[]{:S(2)}, u32[]{:S(2)}) collective-permute-start(bf16[4,128,1024]{1,2,0:T(8,128)(2,1)S(1)} %bitcast.71), channel_id=1, source_target_pairs={{0,1},{1,2},{2,3},{4,5},{5,6},{6,7},{8,9},{9,10},{10,11},{12,13},{... | collective-permute-start | bytes 3145736 | tf_op jit(solution)/shard_map/ppermute | solution.py:30
  32.7 1.3 %collective-permute-start.1 = (bf16[4,128,1024]{1,2,0:T(8,128)(2,1)S(1)}, bf16[4,128,1024]{1,2,0:T(8,128)(2,1)S(1)}, u32[]{:S(2)}, u32[]{:S(2)}) collective-permute-start(bf16[4,128,1024]{1,2,0:T(8,128)(2,1)S(1)} %bitcast.72), channel_id=1, source_target_pairs={{1,0},{2,1},{3,2},{5,4},{6,5},{7,6},{9,8},{10,9},{11,10},{13,12},{... | collective-permute-start | bytes 3145736 | tf_op jit(solution)/shard_map/ppermute | solution.py:31
  34.0 19.5 %collective-permute-done = bf16[4,128,1024]{1,2,0:T(8,128)(2,1)S(1)} collective-permute-done((bf16[4,128,1024]{1,2,0:T(8,128)(2,1)S(1)}, bf16[4,128,1024]{1,2,0:T(8,128)(2,1)S(1)}, u32[]{:S(2)}, u32[]{:S(2)}) %collective-permute-start) | collective-permute-done | bytes 1048608 | tf_op jit(solution)/shard_map/ppermute | solution.py:30
  53.5 4.2 %collective-permute-done.1 = bf16[4,128,1024]{1,2,0:T(8,128)(2,1)S(1)} collective-permute-done((bf16[4,128,1024]{1,2,0:T(8,128)(2,1)S(1)}, bf16[4,128,1024]{1,2,0:T(8,128)(2,1)S(1)}, u32[]{:S(2)}, u32[]{:S(2)}) %collective-permute-start.1) | collective-permute-done | bytes 1048608 | tf_op jit(solution)/shard_map/ppermute | solution.py:31
  57.7 0.4 pad_maximum_fusion
  58.1 2.9 %copy.16 = bf16[12,128,1024]{2,1,0:T(8,128)(2,1)} copy(bf16[12,128,1024]{1,2,0:T(8,128)(2,1)S(1)} %pad_maximum_fusion) | data formatting | bytes 6291456 | tf_op jit(solution)/shard_map/concatenate | solution.py:32
  61.0 0.0 copy-start.2
  61.0 0.0 copy-start.3
  61.0 0.0 all-gather.3.cloned.1.call-update
  61.0 0.6 copy-done.2
  61.7 0.7 fusion.35
  72.2 0.7 fusion.31
  72.9 0.1 compare_reduce_fusion
  73.0 0.0 copy-done.3
  73.0 0.0 copy-done
  73.0 0.3 fusion.28
  73.3 0.7 fusion.34
  73.9 3.0 %all-gather.3.cloned.1.call-done = bf16[24,128,1024]{2,1,0:T(8,128)(2,1)} async-done(((bf16[12,128,1024]{2,1,0:T(8,128)(2,1)}), bf16[24,128,1024]{2,1,0:T(8,128)(2,1)}) %all-gather.3.cloned.1.call-update) | async-done | bytes 6291472 | tf_op jit(solution)/shard_map/all_gather | solution.py:53
  76.9 19.0 %fusion.1 = bf16[1,1,4,128,1024]{4,3,2,1,0:T(8,128)(2,1)} fusion(bf16[2,12,128,1024]{3,2,1,0:T(8,128)(2,1)} %bitcast.70, s32[]{:T(128)S(6)} %add.344, s32[]{:T(128)S(6)} %select_n.52, s32[]{:T(128)S(6)} %select_n.51, s32[]{:T(128)S(6)} %select_n.50, s32[]{:T(128)S(6)} %select_n.49, s32[]{:T(128)S(6)} %select_n.48, s32[]{:T(128)S(6)} %select_n.47, ...), kind=kLoop, calls=%fused_computation.3 | loop fusion | flops 25690112 | bytes 17829988 | tf_op jit(solution)/shard_map/convert_element_type | solution.py:70
  (3 shorter events, 0.0 us)
Async XLA Ops:
  6.5 66.5 %copy-start = (f32[4,8]{1,0:T(4,128)S(1)}, f32[4,8]{1,0:T(4,128)}, u32[]{:S(2)}) copy-start(f32[4,8]{1,0:T(4,128)} %param.10) | copy-start | bytes 388
  6.5 1.6 %copy-start.1 = (bf16[1,1,1,512,1024]{4,3,2,1,0:T(8,128)(2,1)S(1)}, bf16[1,1,1,512,1024]{4,3,2,1,0:T(8,128)(2,1)}, u32[]{:S(2)}) copy-start(bf16[1,1,1,512,1024]{4,3,2,1,0:T(8,128)(2,1)} %param.6) | copy-start | bytes 3145732
  6.5 70.4 %all-gather.3.cloned.1.call-start = ((), (), s32[]{:S(2)}) async-start(), calls=%async_computation.1 | async-start | bytes 9437184 | tf_op jit(solution)/shard_map/all_gather | solution.py:53
  29.1 24.4 %collective-permute-start = (bf16[4,128,1024]{1,2,0:T(8,128)(2,1)S(1)}, bf16[4,128,1024]{1,2,0:T(8,128)(2,1)S(1)}, u32[]{:S(2)}, u32[]{:S(2)}) collective-permute-start(bf16[4,128,1024]{1,2,0:T(8,128)(2,1)S(1)} %bitcast.71), channel_id=1, source_target_pairs={{0,1},{1,2},{2,3},{4,5},{5,6},{6,7},{8,9},{9,10},{10,11},{12,13},{... | collective-permute-start | bytes 3145736 | tf_op jit(solution)/shard_map/ppermute | solution.py:30
  32.7 25.0 %collective-permute-start.1 = (bf16[4,128,1024]{1,2,0:T(8,128)(2,1)S(1)}, bf16[4,128,1024]{1,2,0:T(8,128)(2,1)S(1)}, u32[]{:S(2)}, u32[]{:S(2)}) collective-permute-start(bf16[4,128,1024]{1,2,0:T(8,128)(2,1)S(1)} %bitcast.72), channel_id=1, source_target_pairs={{1,0},{2,1},{3,2},{5,4},{6,5},{7,6},{9,8},{10,9},{11,10},{13,12},{... | collective-permute-start | bytes 3145736 | tf_op jit(solution)/shard_map/ppermute | solution.py:31
  61.0 0.7 copy-start.2
  61.0 12.0 %copy-start.3 = (s32[4]{0:T(128)S(1)}, s32[4]{0:T(128)}, u32[]{:S(2)}) copy-start(s32[4]{0:T(128)} %param.8) | copy-start | bytes 52
Sparse Core Ops, SparseCore 0:
  61.2 15.7 all-gather.2
